TPU v7x, 512 devices: a whole 4x8x8 slice. The times are simulated.
512 devices in a mesh: section: 4 (over x), rep: 128 (over y, z, core).
Axes of the slice: x: 4, y: 8, z: 8, core: 2. Of those that a mesh axis runs over, the one named last changes fastest.
Arguments:
- tile_features: bfloat16 [256, 16, 16, 512], P('rep'), may hold values from -6 to 6
- patches: bfloat16 [256, 16, 16, 768], P('rep'), may hold values from -6 to 6
- det_kernel: float32 [4, 7, 7, 512], P('section'), may hold values from -0.875 to 0.875
- det_gain: float32 [4, 512], P('section'), may hold values from 0.1 to 1.9
- det_in: bfloat16 [4, 512, 2048], P('section', None, 'rep'), may hold values from -0.25 to 0.25
- det_out: bfloat16 [4, 2048, 512], P('section', 'rep'), may hold values from -0.125 to 0.125
- det_scale: float32 [4, 512], P('section'), may hold values from 0.3 to 1.5
- cls_embed: bfloat16 [768, 1024], P(None, 'section'), may hold values from -0.21875 to 0.21875
- cls_merge: bfloat16 [512, 1024], P(None, 'section'), may hold values from -0.25 to 0.25
- cls_pos: bfloat16 [196, 1024], P(None, 'section'), may hold values from -3 to 3
- cls_qkv: bfloat16 [1024, 3, 512], P(None, None, 'section'), may hold values from -1.5 to 1.5
- cls_out: bfloat16 [512, 1024], P('section'), may hold values from -0.25 to 0.25
- cls_gain: float32 [2, 1024], replicated, may hold values from 0.1 to 1.9
- crop_plan: int32 [128, 4, 3, 3], P('rep'), may hold values from 0 to 2, as said below
- slot_from: int32 [128, 4], P('rep'), may hold values from 0 to 3, as said below
Outputs:
- crop_class: float32 [128, 4, 1024], P('rep', 'section')
Inputs may be any that keep to these rules, and one draw needn't show every extreme that they name: `crop_plan`: each entry is a micro-batch below 2 followed by a top and a left patch offset of 0 to 2; records that no slot names are arbitrary. `slot_from`: 0 marks an empty slot, 1 a crop from the replica one index lower, 2 the replica's own, 3 one from the replica one index higher; the first replica never has 1 and the last never has 3.
All inputs are finite; a program needn't handle non-finite values.
Results may differ from a plain program's by a relative error of at most 0.004.
Values may be sent and summed in bfloat16 or wider, within the bound.
No kernel may reach another device: no remote copies, remote signals or barrier semaphores. Data moves between devices by JAX's collectives and lax.ppermute only.
A program may use at most 64 MiB of HBM per device.

v0:
```python
import math
import jax
import jax.numpy as jnp
from jax import lax
from jax.sharding import PartitionSpec as P

HEAD_DIM = 64
TILE = 16
CROP = 14
epsilon = 1e-06


def passed_along(block, axis, distance):
    devices = range(lax.axis_size(axis))
    route = [(i - distance, i) for i in devices if i - distance in devices]
    return lax.ppermute(block, axis, route)


def spread(value, axis, source):
    kept = jnp.where(lax.axis_index(axis) == source, value, 0).astype(value.dtype)
    return lax.psum(kept, axis)


def padded_2(block, sides, width):
    for axis, dim in sides:
        count = lax.axis_size(axis)
        forward = [(i, i + 1) for i in range(count - 1)]
        backward = [(target, source) for source, target in forward]
        low = lax.ppermute(
            lax.slice_in_dim(block, block.shape[dim] - width, None, axis=dim), axis, forward
        )
        high = lax.ppermute(lax.slice_in_dim(block, 0, width, axis=dim), axis, backward)
        block = jnp.concatenate([low, block, high], axis=dim)
    return block


def layer_norm(values, gain_row):
    row_mean = jnp.mean(values, axis=-1, keepdims=True)
    centred = values - row_mean
    row_var = jnp.mean(centred * centred, axis=-1, keepdims=True)
    return centred * lax.rsqrt(row_var + epsilon) * gain_row


def detector_block(tile_rows, kernel, gain_row, in_weight, out_weight, scale_row):
    widened = tile_rows.astype(jnp.float32)
    padded = jnp.pad(widened, ((3, 3), (3, 3), (0, 0)))
    conv = jnp.zeros_like(widened)
    for row_shift in range(7):
        for col_shift in range(7):
            conv = (
                conv
                + padded[row_shift : row_shift + TILE, col_shift : col_shift + TILE]
                * kernel[row_shift, col_shift]
            )
    normed = layer_norm(conv, gain_row).astype(jnp.bfloat16).reshape(TILE * TILE, -1)
    hidden = jax.nn.gelu(jnp.dot(normed, in_weight, preferred_element_type=jnp.float32)).astype(
        jnp.bfloat16
    )
    update = jnp.dot(hidden, out_weight, preferred_element_type=jnp.float32).reshape(widened.shape)
    return (widened + scale_row * update).astype(jnp.bfloat16)


def per_device(
    tile_features,
    patches,
    det_kernel,
    det_gain,
    det_in,
    det_out,
    det_scale,
    cls_embed,
    cls_merge,
    cls_pos,
    cls_qkv,
    cls_out,
    cls_gain,
    crop_plan,
    slot_from,
):
    sections = lax.axis_size("section")
    section_num = lax.axis_index("section")
    micro_count = tile_features.shape[0]
    in_whole, out_whole = (
        lax.all_gather(det_in, "rep", axis=2, tiled=True),
        lax.all_gather(det_out, "rep", axis=1, tiled=True),
    )
    kernel = det_kernel[0]
    gain_row = det_gain[0]
    scale_row = det_scale[0]
    in_weight = in_whole[0]
    out_weight = out_whole[0]

    def run_block(operand_tile):
        return detector_block(operand_tile, kernel, gain_row, in_weight, out_weight, scale_row)

    def skip_block(operand_tile):
        return jnp.zeros_like(operand_tile)

    def tick(tick_index, loop_state):
        incoming, finals = loop_state
        micro_num = tick_index - section_num
        is_valid = (micro_num >= 0) & (micro_num < micro_count)
        clipped = jnp.clip(micro_num, 0, micro_count - 1)
        fresh_tile = lax.dynamic_index_in_dim(tile_features, clipped, 0, keepdims=False)
        operand = jnp.where(section_num == 0, fresh_tile, incoming)
        result = lax.cond(is_valid, run_block, skip_block, operand)
        stored = lax.dynamic_update_index_in_dim(finals, result, clipped, 0)
        finals = jnp.where(is_valid & (section_num == sections - 1), stored, finals)
        incoming = passed_along(result, "section", 1)
        return (incoming, finals)

    start_state = (
        jnp.zeros(tile_features.shape[1:], jnp.bfloat16),
        jnp.zeros(tile_features.shape, jnp.bfloat16),
    )
    unused_tile, finals = lax.fori_loop(0, micro_count + sections - 1, tick, start_state)
    finals = spread(finals, "section", sections - 1)
    pixel_width = patches.shape[3]
    feat_width = finals.shape[3]
    full_width = cls_gain.shape[1]
    local_width = cls_embed.shape[1]
    local_heads = cls_qkv.shape[2] // HEAD_DIM
    qkv_flat = cls_qkv.reshape(cls_qkv.shape[0], -1)
    gain_first = lax.dynamic_slice_in_dim(cls_gain[0], section_num * local_width, local_width)
    slot_plan = crop_plan[0]
    source = lax.dynamic_index_in_dim(slot_from[0], section_num, 0, keepdims=False)
    zero_index = jnp.int32(0)

    def cut_crop(record):
        pixel_rows = lax.dynamic_slice(
            patches, (record[0], record[1], record[2], zero_index), (1, CROP, CROP, pixel_width)
        ).reshape(CROP * CROP, pixel_width)
        feat_rows = lax.dynamic_slice(
            finals, (record[0], record[1], record[2], zero_index), (1, CROP, CROP, feat_width)
        ).reshape(CROP * CROP, feat_width)
        return (pixel_rows, feat_rows)

    pixel_rows, feat_rows = jax.vmap(cut_crop)(slot_plan.reshape(-1, 3))
    count = pixel_rows.shape[0]
    widened = (
        jnp.einsum("crp,pd->crd", pixel_rows, cls_embed, preferred_element_type=jnp.float32)
        + jnp.einsum("crp,pd->crd", feat_rows, cls_merge, preferred_element_type=jnp.float32)
        + cls_pos.astype(jnp.float32)[None]
    )
    row_sum, row_square = lax.psum(
        (jnp.sum(widened, axis=-1), jnp.sum(widened * widened, axis=-1)), "section"
    )
    row_mean = row_sum / full_width
    row_var = row_square / full_width - row_mean * row_mean
    attn_part = (
        (widened - row_mean[..., None]) * lax.rsqrt(row_var[..., None] + epsilon) * gain_first
    ).astype(jnp.bfloat16)
    attn_in = lax.all_gather(attn_part, "section", axis=2, tiled=True)
    qkv = jnp.einsum("crd,de->cre", attn_in, qkv_flat, preferred_element_type=jnp.float32).astype(
        jnp.bfloat16
    )
    qkv = qkv.reshape(count, CROP * CROP, 3, local_heads, HEAD_DIM)
    query_rows = qkv[:, :, 0]
    key_rows = qkv[:, :, 1]
    value_rows = qkv[:, :, 2]
    scores = jnp.einsum(
        "cqhd,ckhd->chqk", query_rows, key_rows, preferred_element_type=jnp.float32
    ) * (1.0 / math.sqrt(HEAD_DIM))
    top_score = jnp.max(scores, axis=-1, keepdims=True)
    weights = jnp.exp(scores - top_score)
    probs = (weights / jnp.sum(weights, axis=-1, keepdims=True)).astype(jnp.bfloat16)
    context = jnp.einsum(
        "chqk,ckhd->cqhd", probs, value_rows, preferred_element_type=jnp.float32
    ).astype(jnp.bfloat16)
    context_mean = jnp.mean(context.reshape(count, CROP * CROP, -1).astype(jnp.float32), axis=1)
    context_term = jnp.dot(
        context_mean, cls_out.astype(jnp.float32), precision=lax.Precision.HIGHEST
    )
    token_mean = jnp.mean(widened, axis=1)
    placed = lax.dynamic_update_slice_in_dim(
        jnp.zeros((count, full_width), jnp.float32), token_mean, section_num * local_width, 1
    )
    terms = (placed + context_term).reshape(sections, -1)
    pooled = lax.psum_scatter(terms, "section", scatter_dimension=0, tiled=True).reshape(
        -1, full_width
    )
    results = layer_norm(pooled, cls_gain[1])
    outgoing_results = jnp.stack([results[0], results[2]], axis=0)
    extended_results = padded_2(outgoing_results, (("rep", 0),), 1)
    result = jnp.where(
        source == 1, extended_results[0], jnp.where(source == 3, extended_results[3], results[1])
    )
    result = jnp.where(source == 0, jnp.zeros_like(result), result)
    return result[None, None, :]


def solution(mesh):
    return jax.shard_map(
        per_device,
        mesh=mesh,
        in_specs=(
            P("rep", None, None, None),
            P("rep", None, None, None),
            P("section", None, None, None),
            P("section", None),
            P("section", None, "rep"),
            P("section", "rep", None),
            P("section", None),
            P(None, "section"),
            P(None, "section"),
            P(None, "section"),
            P(None, None, "section"),
            P("section", None),
            P(),
            P("rep", None, None, None),
            P("rep", None),
        ),
        out_specs=P("rep", "section", None),
        check_vma=False,
    )
```

profile of v0, /device:TPU:32, one launch (start us, length us, event | category | flops | bytes accessed | tf_op | source)
XLA Modules:
  0.0 480.8 jit_solution(15910834706224890067)
XLA Ops:
  8.1 0.8 copy.37
  9.0 0.9 copy.64
  9.9 52.1 %while.18 = (s32[]{:T(128)}, bf16[2,16,16,768]{3,2,1,0:T(8,128)(2,1)}, s32[12,4]{0,1:T(4,128)S(1)}, bf16[12,1,14,14,768]{4,3,2,1,0:T(8,128)(2,1)}, s32[]{:T(128)}) while((s32[]{:T(128)}, bf16[2,16,16,768]{3,2,1,0:T(8,128)(2,1)}, s32[12,4]{0,1:T(4,128)S(1)}, bf16[12,1,14,14,768]{4,3,2,1,0:T(8,128)(2,1)}, s32[]{:T(128)}) %tuple.126), condition=%wide.while_cond, body=%wide.while_body.sunk | while | flops 2 | bytes 690297 | solution.py:130
  10.6 3.7 bitcast_dynamic-update-slice_fusion.2
  14.9 3.7 bitcast_dynamic-update-slice_fusion.2
  19.2 3.7 bitcast_dynamic-update-slice_fusion.2
  23.6 3.7 bitcast_dynamic-update-slice_fusion.2
  27.9 3.7 bitcast_dynamic-update-slice_fusion.2
  32.3 3.7 bitcast_dynamic-update-slice_fusion.2
  36.6 3.7 bitcast_dynamic-update-slice_fusion.2
  41.0 3.7 bitcast_dynamic-update-slice_fusion.2
  45.3 3.7 bitcast_dynamic-update-slice_fusion.2
  49.6 3.7 bitcast_dynamic-update-slice_fusion.2
  54.0 3.7 bitcast_dynamic-update-slice_fusion.2
  58.3 3.7 bitcast_dynamic-update-slice_fusion.2
  62.0 34.7 %all-gather.4.cloned.1.call-done = bf16[1,512,2048]{1,2,0:T(8,128)(2,1)} async-done(((bf16[1,512,16]{1,2,0:T(8,128)(2,1)}), bf16[1,512,2048]{1,2,0:T(8,128)(2,1)}) %all-gather.4.cloned.1.call-update) | async-done | bytes 2097168 | tf_op jit(solution)/shard_map/all_gather | solution.py:84
  96.7 4.0 copy.39
  100.7 79.0 %all-gather.6.cloned.1.call-done = bf16[1,2048,512]{2,1,0:T(8,128)(2,1)} async-done(((bf16[1,16,512]{2,1,0:T(8,128)(2,1)}), bf16[1,2048,512]{2,1,0:T(8,128)(2,1)}) %all-gather.6.cloned.1.call-update) | async-done | bytes 2097168 | tf_op jit(solution)/shard_map/all_gather | solution.py:85
  179.7 84.6 %while.17 = (s32[]{:T(128)}, bf16[16,16,512]{2,1,0:T(8,128)(2,1)S(1)}, bf16[2,16,16,512]{3,2,1,0:T(8,128)(2,1)S(1)}, s32[]{:T(128)}, pred[]{:T(512)}, /*index=5*...) while((s32[]{:T(128)}, ...), condition=%wide.region_5.6_spmd, body=%wide.region_0.5_spmd.sunk | while | flops 1093009664 | bytes 12373336 | solution.py:116
  179.8 10.3 %conditional.2 = (bf16[16,16,512]{2,1,0:T(8,128)(2,1)}, bf16[1,16,16,512]{3,2,1,0:T(8,128)(2,1)S(1)}) conditional(s32[]{:T(128)} %convert_element_type.74, () %tuple.120, (pred[]{:T(512)}, bf16[2,16,16,512]{3,2,1,0:T(8,128)(2,1)S(1)}, s32[]{:T(128)}, bf16[16,16,512]{2,1,0:T(8,128)(2,1)S(1)}, f32[1,512]{1,0:T(1,128)S(1)}, ...), branch_computations={%region_1.1_spmd, %region_2.4_spmd} | conditional | flops 1092878592 | bytes 10538005 | solution.py:106
  180.0 4.2 fusion.129
  184.6 3.8 fusion.8
  188.4 0.8 add_convert_fusion
  189.2 0.9 copy.68
  190.1 1.3 collective-permute-start
  191.5 6.5 %collective-permute-done = bf16[16,16,512]{2,1,0:T(8,128)(2,1)S(1)} collective-permute-done((bf16[16,16,512]{2,1,0:T(8,128)(2,1)}, bf16[16,16,512]{2,1,0:T(8,128)(2,1)S(1)}, u32[]{:S(2)}, u32[]{:S(2)}) %collective-permute-start) | collective-permute-done | bytes 262176 | tf_op jit(solution)/shard_map/while/body/eval_jaxpr/ppermute | solution.py:16
  198.0 10.3 %conditional.2 = (bf16[16,16,512]{2,1,0:T(8,128)(2,1)}, bf16[1,16,16,512]{3,2,1,0:T(8,128)(2,1)S(1)}) conditional(s32[]{:T(128)} %convert_element_type.74, () %tuple.120, (pred[]{:T(512)}, bf16[2,16,16,512]{3,2,1,0:T(8,128)(2,1)S(1)}, s32[]{:T(128)}, bf16[16,16,512]{2,1,0:T(8,128)(2,1)S(1)}, f32[1,512]{1,0:T(1,128)S(1)}, ...), branch_computations={%region_1.1_spmd, %region_2.4_spmd} | conditional | flops 1092878592 | bytes 10538005 | solution.py:106
  198.1 4.2 fusion.129
  202.8 3.8 fusion.8
  206.6 0.8 add_convert_fusion
  207.4 0.9 copy.68
  208.3 4.3 collective-permute-start
  212.7 5.7 %collective-permute-done = bf16[16,16,512]{2,1,0:T(8,128)(2,1)S(1)} collective-permute-done((bf16[16,16,512]{2,1,0:T(8,128)(2,1)}, bf16[16,16,512]{2,1,0:T(8,128)(2,1)S(1)}, u32[]{:S(2)}, u32[]{:S(2)}) %collective-permute-start) | collective-permute-done | bytes 262176 | tf_op jit(solution)/shard_map/while/body/eval_jaxpr/ppermute | solution.py:16
  218.4 0.7 conditional.2
  218.4 0.7 broadcast.139
  219.2 13.9 %collective-permute-start = (bf16[16,16,512]{2,1,0:T(8,128)(2,1)}, bf16[16,16,512]{2,1,0:T(8,128)(2,1)S(1)}, u32[]{:S(2)}, u32[]{:S(2)}) collective-permute-start(bf16[16,16,512]{2,1,0:T(8,128)(2,1)} %get-tuple-element.531), channel_id=1, source_target_pairs={{0,128},{128,256},{256,384},{1,129},{129,257},{257,385},{2,130},{1... | collective-permute-start | bytes 786440 | tf_op jit(solution)/shard_map/while/body/eval_jaxpr/ppermute | solution.py:16
  233.1 4.8 %collective-permute-done = bf16[16,16,512]{2,1,0:T(8,128)(2,1)S(1)} collective-permute-done((bf16[16,16,512]{2,1,0:T(8,128)(2,1)}, bf16[16,16,512]{2,1,0:T(8,128)(2,1)S(1)}, u32[]{:S(2)}, u32[]{:S(2)}) %collective-permute-start) | collective-permute-done | bytes 262176 | tf_op jit(solution)/shard_map/while/body/eval_jaxpr/ppermute | solution.py:16
  237.9 0.7 conditional.2
  237.9 0.7 broadcast.139
  238.7 4.3 collective-permute-start
  243.1 4.1 collective-permute-done
  247.2 0.7 conditional.2
  247.2 0.7 broadcast.139
  247.9 12.2 %collective-permute-start = (bf16[16,16,512]{2,1,0:T(8,128)(2,1)}, bf16[16,16,512]{2,1,0:T(8,128)(2,1)S(1)}, u32[]{:S(2)}, u32[]{:S(2)}) collective-permute-start(bf16[16,16,512]{2,1,0:T(8,128)(2,1)} %get-tuple-element.531), channel_id=1, source_target_pairs={{0,128},{128,256},{256,384},{1,129},{129,257},{257,385},{2,130},{1... | collective-permute-start | bytes 786440 | tf_op jit(solution)/shard_map/while/body/eval_jaxpr/ppermute | solution.py:16
  260.2 4.1 collective-permute-done
  264.3 1.5 broadcast_select_fusion
  266.1 6.0 %reshape.115 = bf16[12,196,768]{2,1,0:T(8,128)(2,1)} reshape(bf16[12,1,14,14,768]{4,3,2,1,0:T(8,128)(2,1)} %get-tuple-element.289) | data formatting | bytes 7225344 | tf_op jit(solution)/shard_map/vmap()/reshape | solution.py:132
  272.2 3.2 fusion.123
  275.3 52.9 %all-reduce.5.cloned.1.call-done = bf16[2,16,16,512]{3,0,2,1:T(2,128)(2,1)} async-done(((bf16[2,16,16,512]{3,0,2,1:T(2,128)(2,1)}), bf16[2,16,16,512]{3,0,2,1:T(2,128)(2,1)}) %all-reduce.5.cloned.1.call-update) | async-done | bytes 524304 | tf_op jit(solution)/shard_map/psum | solution.py:21
  328.2 12.1 %gather_fusion = bf16[12,14,14,512]{3,0,2,1:T(8,128)(2,1)} fusion(bf16[2,16,16,512]{3,0,2,1:T(2,128)(2,1)} %all-reduce.5.cloned.1.call-done, s32[12]{0:T(128)S(1)} %get-tuple-element.423), kind=kCustom, calls=%fused_computation | custom fusion | bytes 4817088 | tf_op jit(solution)/shard_map/vmap()/gather | solution.py:133
  340.3 6.5 %fusion.128 = (f32[12,256]{1,0:T(8,128)S(1)}, f32[12,196]{1,0:T(8,128)S(1)}, f32[12,196]{1,0:T(8,128)S(1)}, f32[12,196,256]{2,1,0:T(8,128)}) fusion(f32[196,256]{1,0:T(8,128)S(1)} %convert_element_type.50, f32[12,196,256]{2,1,0:T(8,128)S(1)} %fusion.123, bf16[512,256]{1,0:T(8,128)(2,1)S(1)} %copy-done.9, bf16[12,196,512]{2,0,1:T(8,128)(2,1)} %bitcast.131), kind=kOutput, calls=%fused_computation.214 | convolution fusion | flops 620167552 | bytes 7719296 | tf_op jit(solution)/shard_map/crp,pd->crd/dot_general | solution.py:142
  346.7 16.1 %all-reduce.2 = (f32[12,196]{1,0:T(8,128)S(1)}, f32[12,196]{1,0:T(8,128)S(1)}) all-reduce(f32[12,196]{1,0:T(8,128)S(1)} %get-tuple-element.327, f32[12,196]{1,0:T(8,128)S(1)} %get-tuple-element.328), channel_id=1, replica_groups=mesh['section'=4,'rep'=128] {'section'}, use_global_device_ids=true, to_apply=%region_10.11 | all-reduce | flops 4704 | bytes 37632 | tf_op jit(solution)/shard_map/psum | solution.py:145
  362.8 3.0 multiply_convert_fusion.1
  366.2 1.3 dynamic-slice.12
  367.5 61.6 %all-gather.8.cloned.1.call-done = bf16[12,196,1024]{2,1,0:T(8,128)(2,1)} async-done(((bf16[12,196,256]{2,1,0:T(8,128)(2,1)}), bf16[12,196,1024]{2,1,0:T(8,128)(2,1)}) %all-gather.8.cloned.1.call-update) | async-done | bytes 4816912 | tf_op jit(solution)/shard_map/all_gather | solution.py:153
  429.1 6.4 %convolution_convert_fusion = bf16[12,196,384]{2,1,0:T(8,128)(2,1)} fusion(bf16[12,196,1024]{2,1,0:T(8,128)(2,1)} %all-gather.8.cloned.1.call-done, bf16[1024,384,1]{0,1,2:T(8,128)(2,1)S(1)} %bitcast.133), kind=kOutput, calls=%fused_computation.181 | convolution fusion | flops 1850591232 | bytes 7409664 | tf_op jit(solution)/shard_map/crd,de->cre/dot_general | solution.py:154
  435.6 2.7 copy.44
  438.3 0.8 fusion.122
  439.1 4.1 fusion.137
  443.3 0.8 convert_reduce_fusion
  444.5 16.7 %all-reduce.1 = f32[4,3072]{1,0:T(4,128)S(1)} all-reduce(f32[4,3072]{1,0:T(4,128)S(1)} %reshape.119), channel_id=2, replica_groups=mesh['section'=4,'rep'=128] {'section'}, use_global_device_ids=true, to_apply=%region_15.16.clone | all-reduce | flops 12288 | bytes 98304
  462.3 1.9 collective-permute-start.1
  464.3 7.0 %collective-permute-start.2 = (f32[1,1024]{1,0:T(1,128)S(1)}, f32[1,1024]{1,0:T(1,128)S(1)}, u32[]{:S(2)}, u32[]{:S(2)}) collective-permute-start(f32[1,1024]{1,0:T(1,128)S(1)} %get-tuple-element.417), channel_id=1, source_target_pairs={{1,0},{2,1},{3,2},{4,3},{5,4},{6,5},{7,6},{8,7},{9,8},{10,9},{11,1... | collective-permute-start | bytes 12296 | tf_op jit(solution)/shard_map/ppermute | solution.py:32
  473.1 1.2 fusion.126
  (104 shorter events, 14.0 us)
Async XLA Ops:
  6.5 265.6 %copy-start = (bf16[768,256]{1,0:T(8,128)(2,1)S(1)}, bf16[768,256]{1,0:T(8,128)(2,1)}, u32[]{:S(2)}) copy-start(bf16[768,256]{1,0:T(8,128)(2,1)} %param.26) | copy-start | bytes 1179652
  6.5 90.1 %all-gather.4.cloned.1.call-start = ((), (), s32[]{:S(2)}) async-start(), calls=%async_computation | async-start | bytes 2113536 | tf_op jit(solution)/shard_map/all_gather | solution.py:84
  7.3 172.4 %all-gather.6.cloned.1.call-start = ((), (), s32[]{:S(2)}) async-start(), calls=%async_computation.1 | async-start | bytes 2113536 | tf_op jit(solution)/shard_map/all_gather | solution.py:85
  8.0 320.2 %all-reduce.5.cloned.1.call-start = ((), (), s32[]{:S(2)}) async-start(), calls=%async_computation.2 | async-start | bytes 1048576 | tf_op jit(solution)/shard_map/psum | solution.py:21
  96.7 83.1 %copy-start.1 = (bf16[2,16,16,512]{3,2,1,0:T(8,128)(2,1)S(1)}, bf16[2,16,16,512]{3,2,1,0:T(8,128)(2,1)}, u32[]{:S(2)}) copy-start(bf16[2,16,16,512]{3,2,1,0:T(8,128)(2,1)} %param.19) | copy-start | bytes 1572868
  96.7 83.1 %copy-start.5 = (f32[1,512]{1,0:T(1,128)S(1)}, f32[1,512]{1,0:T(1,128)}, u32[]{:S(2)}) copy-start(f32[1,512]{1,0:T(1,128)} %param.25) | copy-start | bytes 6148
  96.7 83.1 %copy-start.6 = (f32[1,512]{1,0:T(1,128)S(1)}, f32[1,512]{1,0:T(1,128)}, u32[]{:S(2)}) copy-start(f32[1,512]{1,0:T(1,128)} %param.22) | copy-start | bytes 6148
  179.7 86.3 %copy-start.7 = (f32[2,1024]{1,0:T(2,128)S(1)}, f32[2,1024]{1,0:T(2,128)}, u32[]{:S(2)}) copy-start(f32[2,1024]{1,0:T(2,128)} %param.31) | copy-start | bytes 24580
  190.1 7.9 %collective-permute-start = (bf16[16,16,512]{2,1,0:T(8,128)(2,1)}, bf16[16,16,512]{2,1,0:T(8,128)(2,1)S(1)}, u32[]{:S(2)}, u32[]{:S(2)}) collective-permute-start(bf16[16,16,512]{2,1,0:T(8,128)(2,1)} %get-tuple-element.531), channel_id=1, source_target_pairs={{0,128},{128,256},{256,384},{1,129},{129,257},{257,385},{2,130},{1... | collective-permute-start | bytes 786440 | tf_op jit(solution)/shard_map/while/body/eval_jaxpr/ppermute | solution.py:16
  208.3 10.1 %collective-permute-start = (bf16[16,16,512]{2,1,0:T(8,128)(2,1)}, bf16[16,16,512]{2,1,0:T(8,128)(2,1)S(1)}, u32[]{:S(2)}, u32[]{:S(2)}) collective-permute-start(bf16[16,16,512]{2,1,0:T(8,128)(2,1)} %get-tuple-element.531), channel_id=1, source_target_pairs={{0,128},{128,256},{256,384},{1,129},{129,257},{257,385},{2,130},{1... | collective-permute-start | bytes 786440 | tf_op jit(solution)/shard_map/while/body/eval_jaxpr/ppermute | solution.py:16
  219.2 18.8 %collective-permute-start = (bf16[16,16,512]{2,1,0:T(8,128)(2,1)}, bf16[16,16,512]{2,1,0:T(8,128)(2,1)S(1)}, u32[]{:S(2)}, u32[]{:S(2)}) collective-permute-start(bf16[16,16,512]{2,1,0:T(8,128)(2,1)} %get-tuple-element.531), channel_id=1, source_target_pairs={{0,128},{128,256},{256,384},{1,129},{129,257},{257,385},{2,130},{1... | collective-permute-start | bytes 786440 | tf_op jit(solution)/shard_map/while/body/eval_jaxpr/ppermute | solution.py:16
  238.7 8.5 %collective-permute-start = (bf16[16,16,512]{2,1,0:T(8,128)(2,1)}, bf16[16,16,512]{2,1,0:T(8,128)(2,1)S(1)}, u32[]{:S(2)}, u32[]{:S(2)}) collective-permute-start(bf16[16,16,512]{2,1,0:T(8,128)(2,1)} %get-tuple-element.531), channel_id=1, source_target_pairs={{0,128},{128,256},{256,384},{1,129},{129,257},{257,385},{2,130},{1... | collective-permute-start | bytes 786440 | tf_op jit(solution)/shard_map/while/body/eval_jaxpr/ppermute | solution.py:16
  247.9 16.4 %collective-permute-start = (bf16[16,16,512]{2,1,0:T(8,128)(2,1)}, bf16[16,16,512]{2,1,0:T(8,128)(2,1)S(1)}, u32[]{:S(2)}, u32[]{:S(2)}) collective-permute-start(bf16[16,16,512]{2,1,0:T(8,128)(2,1)} %get-tuple-element.531), channel_id=1, source_target_pairs={{0,128},{128,256},{256,384},{1,129},{129,257},{257,385},{2,130},{1... | collective-permute-start | bytes 786440 | tf_op jit(solution)/shard_map/while/body/eval_jaxpr/ppermute | solution.py:16
  265.8 163.3 %all-gather.8.cloned.1.call-start = ((), (), s32[]{:S(2)}) async-start(), calls=%async_computation.3 | async-start | bytes 6144000 | tf_op jit(solution)/shard_map/all_gather | solution.py:153
  266.1 6.0 %copy-start.4 = (bf16[196,256]{1,0:T(8,128)(2,1)S(1)}, bf16[196,256]{1,0:T(8,128)(2,1)}, u32[]{:S(2)}) copy-start(bf16[196,256]{1,0:T(8,128)(2,1)} %param.28) | copy-start | bytes 301060
  328.2 12.1 %copy-start.9 = (bf16[512,256]{1,0:T(8,128)(2,1)S(1)}, bf16[512,256]{1,0:T(8,128)(2,1)}, u32[]{:S(2)}) copy-start(bf16[512,256]{1,0:T(8,128)(2,1)} %param.27) | copy-start | bytes 786436
  362.8 3.1 copy-start.2
  443.3 1.0 copy-start.3
  443.3 28.0 %copy-start.8 = (s32[1,4]{1,0:T(1,128)S(1)}, s32[1,4]{1,0:T(1,128)}, u32[]{:S(2)}) copy-start(s32[1,4]{1,0:T(1,128)} %param.33) | copy-start | bytes 52
  462.3 10.8 %collective-permute-start.1 = (f32[1,1024]{1,0:T(1,128)S(1)}, f32[1,1024]{1,0:T(1,128)S(1)}, u32[]{:S(2)}, u32[]{:S(2)}) collective-permute-start(f32[1,1024]{1,0:T(1,128)S(1)} %get-tuple-element.418), channel_id=1, source_target_pairs={{0,1},{1,2},{2,3},{3,4},{4,5},{5,6},{6,7},{7,8},{8,9},{9,10},{10,1... | collective-permute-start | bytes 12296 | tf_op jit(solution)/shard_map/ppermute | solution.py:29
  464.3 8.9 %collective-permute-start.2 = (f32[1,1024]{1,0:T(1,128)S(1)}, f32[1,1024]{1,0:T(1,128)S(1)}, u32[]{:S(2)}, u32[]{:S(2)}) collective-permute-start(f32[1,1024]{1,0:T(1,128)S(1)} %get-tuple-element.417), channel_id=1, source_target_pairs={{1,0},{2,1},{3,2},{4,3},{5,4},{6,5},{7,6},{8,7},{9,8},{10,9},{11,1... | collective-permute-start | bytes 12296 | tf_op jit(solution)/shard_map/ppermute | solution.py:32
Sparse Core Ops, SparseCore 0:
  10.5 86.1 all-gather.3
  99.8 79.7 all-gather.5
  265.9 62.2 all-reduce.4
  366.0 63.1 all-gather.7
where the time goes:
time: 482 us; the launch traced here: 481 us
  waiting for transfers between devices  255 us (53%)
  local copies, waits for them, and re-layouts  85.6 us (18%)
  starting transfers between devices  45.1 us (9%)
  blocking collectives  32.7 us (7%)
  matrix products  25.5 us (5%)
  other arithmetic  22.2 us (5%)
  between operations  14.8 us (3%)
    all_gather x1, waiting for transfers between devices, per_device(): lax.all_gather(det_out, 'rep', axis=1, tiled=True)  79 us
    all_gather x1, waiting for transfers between devices, per_device(): attn_in = lax.all_gather(attn_part, 'section', axis=2, tiled=True)  61.6 us
    psum x1, waiting for transfers between devices, spread(): return lax.psum(kept, axis)  52.9 us
    gather x36, local copies, waits for them, and re-layouts  52 us
    ppermute x5, starting transfers between devices, passed_along(): return lax.ppermute(block, axis, route)  35.9 us
    all_gather x1, waiting for transfers between devices, per_device(): lax.all_gather(det_in, 'rep', axis=2, tiled=True)  34.7 us
    ppermute x5, waiting for transfers between devices, passed_along(): return lax.ppermute(block, axis, route)  25.1 us
    unnamed x1, blocking collectives  16.7 us
  transfers between devices with their start and end apart: 11, of which 9 were waited for; matrix products, arithmetic and copies ran while one was open for 15% of the time, Pallas kernels for 0%

commit v1 on v0

--- a/solution.py
+++ b/solution.py
@@ -18,7 +18,7 @@
 
 def spread(value, axis, source):
     kept = jnp.where(lax.axis_index(axis) == source, value, 0).astype(value.dtype)
-    return lax.psum(kept, axis)
+    return jnp.sum(lax.all_gather(kept, axis), axis=0)
 
 
 def padded_2(block, sides, width):

time: 482 us -> 491 us (1.019)
  blocking collectives: 32.7 us -> 44.4 us
  waiting for transfers between devices: 255 us -> 250 us
    psum x1 -> x0, waiting for transfers between devices: 52.9 us -> none  [spread(): return lax.psum(kept, axis)]
    all_gather x1, waiting for transfers between devices: 34.7 us -> 86.7 us  [per_device(): lax.all_gather(det_in, 'rep', axis=2, tiled=True)]
    psum x1, blocking collectives: 16.1 us -> 27.8 us  [per_device(): lax.psum((jnp.sum(widened, axis=-1), jnp.sum(widened * widened, axis=-1))...]
  transfers between devices with their start and end apart: 11 -> 11, of which waited for: 9 -> 8; matrix products, arithmetic and copies ran while one was open for 15% -> 15% of each run, Pallas kernels for 0% -> 0%
where the time goes in v1:
time: 491 us; the launch traced here: 489 us
  waiting for transfers between devices  250 us (51%)
  local copies, waits for them, and re-layouts  83.2 us (17%)
  starting transfers between devices  45.2 us (9%)
  blocking collectives  44.4 us (9%)
  matrix products  25.5 us (5%)
  other arithmetic  25.4 us (5%)
  between operations  14.7 us (3%)
    all_gather x1, waiting for transfers between devices, per_device(): lax.all_gather(det_in, 'rep', axis=2, tiled=True)  86.7 us
    all_gather x1, waiting for transfers between devices, per_device(): lax.all_gather(det_out, 'rep', axis=1, tiled=True)  78.9 us
    all_gather x1, waiting for transfers between devices, per_device(): attn_in = lax.all_gather(attn_part, 'section', axis=2, tiled=True)  58.4 us
    gather x36, local copies, waits for them, and re-layouts  52.6 us
    ppermute x5, starting transfers between devices, passed_along(): return lax.ppermute(block, axis, route)  36 us
    psum x1, blocking collectives, per_device(): lax.psum((jnp.sum(widened, axis=-1), jnp.sum(widened * widened, axis=-1))...  27.8 us
    ppermute x5, waiting for transfers between devices, passed_along(): return lax.ppermute(block, axis, route)  25.1 us
    unnamed x1, blocking collectives  16.7 us
  transfers between devices with their start and end apart: 11, of which 8 were waited for; matrix products, arithmetic and copies ran while one was open for 15% of the time, Pallas kernels for 0%

profile of v1, /device:TPU:32, one launch (start us, length us, event | category | flops | bytes accessed | tf_op | source)
XLA Modules:
  0.0 489.2 jit_solution(17423052550032170355)
XLA Ops:
  8.1 0.9 copy.58
  9.0 0.8 copy.33
  9.9 86.7 %all-gather.6.cloned.1.call-done = bf16[1,512,2048]{1,2,0:T(8,128)(2,1)} async-done(((bf16[1,512,16]{1,2,0:T(8,128)(2,1)}), bf16[1,512,2048]{1,2,0:T(8,128)(2,1)}) %all-gather.6.cloned.1.call-update) | async-done | bytes 2097168 | tf_op jit(solution)/shard_map/all_gather | solution.py:84
  96.6 4.1 copy.34
  100.6 78.9 %all-gather.8.cloned.1.call-done = bf16[1,2048,512]{2,1,0:T(8,128)(2,1)} async-done(((bf16[1,16,512]{2,1,0:T(8,128)(2,1)}), bf16[1,2048,512]{2,1,0:T(8,128)(2,1)}) %all-gather.8.cloned.1.call-update) | async-done | bytes 2097168 | tf_op jit(solution)/shard_map/all_gather | solution.py:85
  179.7 84.6 %while.17 = (s32[]{:T(128)}, bf16[16,16,512]{2,1,0:T(8,128)(2,1)S(1)}, bf16[2,16,16,512]{3,2,1,0:T(8,128)(2,1)S(1)}, s32[]{:T(128)}, pred[]{:T(512)}, /*index=5*...) while((s32[]{:T(128)}, ...), condition=%wide.region_5.6_spmd, body=%wide.region_0.5_spmd.sunk | while | flops 1093009664 | bytes 12373336 | solution.py:116
  179.7 10.4 %conditional.2 = (bf16[16,16,512]{2,1,0:T(8,128)(2,1)}, bf16[1,16,16,512]{3,2,1,0:T(8,128)(2,1)S(1)}) conditional(s32[]{:T(128)} %convert_element_type.76, () %tuple.118, (pred[]{:T(512)}, bf16[2,16,16,512]{3,2,1,0:T(8,128)(2,1)S(1)}, s32[]{:T(128)}, bf16[16,16,512]{2,1,0:T(8,128)(2,1)S(1)}, f32[1,512]{1,0:T(1,128)S(1)}, ...), branch_computations={%region_1.1_spmd, %region_2.4_spmd} | conditional | flops 1092878592 | bytes 10538005 | solution.py:106
  179.9 4.2 fusion.129
  184.5 3.8 fusion.8
  188.3 0.8 add_convert_fusion
  189.1 0.9 copy.62
  190.0 1.3 collective-permute-start
  191.4 6.5 %collective-permute-done = bf16[16,16,512]{2,1,0:T(8,128)(2,1)S(1)} collective-permute-done((bf16[16,16,512]{2,1,0:T(8,128)(2,1)}, bf16[16,16,512]{2,1,0:T(8,128)(2,1)S(1)}, u32[]{:S(2)}, u32[]{:S(2)}) %collective-permute-start) | collective-permute-done | bytes 262176 | tf_op jit(solution)/shard_map/while/body/eval_jaxpr/ppermute | solution.py:16
  197.9 10.3 %conditional.2 = (bf16[16,16,512]{2,1,0:T(8,128)(2,1)}, bf16[1,16,16,512]{3,2,1,0:T(8,128)(2,1)S(1)}) conditional(s32[]{:T(128)} %convert_element_type.76, () %tuple.118, (pred[]{:T(512)}, bf16[2,16,16,512]{3,2,1,0:T(8,128)(2,1)S(1)}, s32[]{:T(128)}, bf16[16,16,512]{2,1,0:T(8,128)(2,1)S(1)}, f32[1,512]{1,0:T(1,128)S(1)}, ...), branch_computations={%region_1.1_spmd, %region_2.4_spmd} | conditional | flops 1092878592 | bytes 10538005 | solution.py:106
  198.1 4.2 fusion.129
  202.7 3.8 fusion.8
  206.5 0.8 add_convert_fusion
  207.3 0.9 copy.62
  208.2 4.3 collective-permute-start
  212.6 5.7 %collective-permute-done = bf16[16,16,512]{2,1,0:T(8,128)(2,1)S(1)} collective-permute-done((bf16[16,16,512]{2,1,0:T(8,128)(2,1)}, bf16[16,16,512]{2,1,0:T(8,128)(2,1)S(1)}, u32[]{:S(2)}, u32[]{:S(2)}) %collective-permute-start) | collective-permute-done | bytes 262176 | tf_op jit(solution)/shard_map/while/body/eval_jaxpr/ppermute | solution.py:16
  218.3 0.8 conditional.2
  218.3 0.7 broadcast.139
  219.1 13.8 %collective-permute-start = (bf16[16,16,512]{2,1,0:T(8,128)(2,1)}, bf16[16,16,512]{2,1,0:T(8,128)(2,1)S(1)}, u32[]{:S(2)}, u32[]{:S(2)}) collective-permute-start(bf16[16,16,512]{2,1,0:T(8,128)(2,1)} %get-tuple-element.507), channel_id=1, source_target_pairs={{0,128},{128,256},{256,384},{1,129},{129,257},{257,385},{2,130},{1... | collective-permute-start | bytes 786440 | tf_op jit(solution)/shard_map/while/body/eval_jaxpr/ppermute | solution.py:16
  233.0 4.8 collective-permute-done
  237.8 0.8 conditional.2
  237.8 0.7 broadcast.139
  238.6 4.3 collective-permute-start
  243.0 4.1 collective-permute-done
  247.1 0.8 conditional.2
  247.9 12.2 %collective-permute-start = (bf16[16,16,512]{2,1,0:T(8,128)(2,1)}, bf16[16,16,512]{2,1,0:T(8,128)(2,1)S(1)}, u32[]{:S(2)}, u32[]{:S(2)}) collective-permute-start(bf16[16,16,512]{2,1,0:T(8,128)(2,1)} %get-tuple-element.507), channel_id=1, source_target_pairs={{0,128},{128,256},{256,384},{1,129},{129,257},{257,385},{2,130},{1... | collective-permute-start | bytes 786440 | tf_op jit(solution)/shard_map/while/body/eval_jaxpr/ppermute | solution.py:16
  260.2 4.1 collective-permute-done
  264.3 0.9 broadcast_select_fusion
  265.4 52.6 %while.18 = (s32[]{:T(128)}, bf16[2,16,16,768]{3,2,1,0:T(8,128)(2,1)}, s32[12,4]{0,1:T(4,128)S(1)}, bf16[12,1,14,14,768]{4,3,2,1,0:T(8,128)(2,1)}, s32[]{:T(128)}) while((s32[]{:T(128)}, bf16[2,16,16,768]{3,2,1,0:T(8,128)(2,1)}, s32[12,4]{0,1:T(4,128)S(1)}, bf16[12,1,14,14,768]{4,3,2,1,0:T(8,128)(2,1)}, s32[]{:T(128)}) %tuple.124), condition=%wide.while_cond, body=%wide.while_body.sunk | while | flops 2 | bytes 690297 | solution.py:130
  266.1 3.7 bitcast_dynamic-update-slice_fusion.2
  270.4 3.7 bitcast_dynamic-update-slice_fusion.2
  274.8 3.7 bitcast_dynamic-update-slice_fusion.2
  279.2 3.7 bitcast_dynamic-update-slice_fusion.2
  283.6 3.7 bitcast_dynamic-update-slice_fusion.2
  288.0 3.7 bitcast_dynamic-update-slice_fusion.2
  292.4 3.7 bitcast_dynamic-update-slice_fusion.2
  296.8 3.7 bitcast_dynamic-update-slice_fusion.2
  301.1 3.7 bitcast_dynamic-update-slice_fusion.2
  305.5 3.7 bitcast_dynamic-update-slice_fusion.2
  309.9 3.7 bitcast_dynamic-update-slice_fusion.2
  314.3 3.7 bitcast_dynamic-update-slice_fusion.2
  318.0 6.0 %reshape.115 = bf16[12,196,768]{2,1,0:T(8,128)(2,1)} reshape(bf16[12,1,14,14,768]{4,3,2,1,0:T(8,128)(2,1)} %get-tuple-element.289) | data formatting | bytes 7225344 | tf_op jit(solution)/shard_map/vmap()/reshape | solution.py:132
  324.8 3.2 fusion.123
  328.0 2.9 reduce_sum.95
  330.9 1.6 copy.35
  332.5 7.4 %gather_fusion = bf16[12,14,14,512]{3,0,2,1:T(8,128)(2,1)} fusion(bf16[2,16,16,512]{3,0,2,1:T(2,128)(2,1)S(1)} %copy.35, s32[12]{0:T(128)S(1)} %get-tuple-element.399), kind=kCustom, calls=%fused_computation | custom fusion | bytes 4817088 | tf_op jit(solution)/shard_map/vmap()/gather | solution.py:133
  339.9 6.5 %fusion.128 = (f32[12,256]{1,0:T(8,128)S(1)}, f32[12,196]{1,0:T(8,128)S(1)}, f32[12,196]{1,0:T(8,128)S(1)}, f32[12,196,256]{2,1,0:T(8,128)}) fusion(f32[196,256]{1,0:T(8,128)} %convert_element_type.52, f32[12,196,256]{2,1,0:T(8,128)S(1)} %fusion.123, bf16[512,256]{1,0:T(8,128)(2,1)} %param.27, bf16[12,196,512]{2,0,1:T(8,128)(2,1)} %bitcast.132), kind=kOutput, calls=%fused_computation.214 | convolution fusion | flops 620167552 | bytes 7719296 | tf_op jit(solution)/shard_map/crp,pd->crd/dot_general | solution.py:142
  346.4 27.8 %all-reduce.2 = (f32[12,196]{1,0:T(8,128)S(1)}, f32[12,196]{1,0:T(8,128)S(1)}) all-reduce(f32[12,196]{1,0:T(8,128)S(1)} %get-tuple-element.303, f32[12,196]{1,0:T(8,128)S(1)} %get-tuple-element.304), channel_id=1, replica_groups=mesh['section'=4,'rep'=128] {'section'}, use_global_device_ids=true, to_apply=%region_10.11 | all-reduce | flops 4704 | bytes 37632 | tf_op jit(solution)/shard_map/psum | solution.py:145
  374.2 3.0 multiply_convert_fusion.1
  377.6 1.3 dynamic-slice.12
  378.9 58.4 %all-gather.10.cloned.1.call-done = bf16[12,196,1024]{2,1,0:T(8,128)(2,1)} async-done(((bf16[12,196,256]{2,1,0:T(8,128)(2,1)}), bf16[12,196,1024]{2,1,0:T(8,128)(2,1)}) %all-gather.10.cloned.1.call-update) | async-done | bytes 4816912 | tf_op jit(solution)/shard_map/all_gather | solution.py:153
  437.3 6.4 %convolution_convert_fusion = bf16[12,196,384]{2,1,0:T(8,128)(2,1)} fusion(bf16[12,196,1024]{2,1,0:T(8,128)(2,1)} %all-gather.10.cloned.1.call-done, bf16[1024,384,1]{0,1,2:T(8,128)(2,1)S(1)} %bitcast.135), kind=kOutput, calls=%fused_computation.181 | convolution fusion | flops 1850591232 | bytes 7409664 | tf_op jit(solution)/shard_map/crd,de->cre/dot_general | solution.py:154
  443.7 2.7 copy.39
  446.4 0.8 fusion.122
  447.3 4.1 fusion.137
  451.5 0.8 convert_reduce_fusion
  452.7 16.7 %all-reduce.1 = f32[4,3072]{1,0:T(4,128)S(1)} all-reduce(f32[4,3072]{1,0:T(4,128)S(1)} %reshape.119), channel_id=3, replica_groups=mesh['section'=4,'rep'=128] {'section'}, use_global_device_ids=true, to_apply=%region_15.16.clone | all-reduce | flops 12288 | bytes 98304
  470.5 1.9 collective-permute-start.1
  472.4 7.0 %collective-permute-start.2 = (f32[1,1024]{1,0:T(1,128)S(1)}, f32[1,1024]{1,0:T(1,128)S(1)}, u32[]{:S(2)}, u32[]{:S(2)}) collective-permute-start(f32[1,1024]{1,0:T(1,128)S(1)} %get-tuple-element.393), channel_id=1, source_target_pairs={{1,0},{2,1},{3,2},{4,3},{5,4},{6,5},{7,6},{8,7},{9,8},{10,9},{11,1... | collective-permute-start | bytes 12296 | tf_op jit(solution)/shard_map/ppermute | solution.py:32
  481.4 1.3 fusion.126
  (104 shorter events, 15.4 us)
Async XLA Ops:
  6.5 318.2 %copy-start = (bf16[768,256]{1,0:T(8,128)(2,1)S(1)}, bf16[768,256]{1,0:T(8,128)(2,1)}, u32[]{:S(2)}) copy-start(bf16[768,256]{1,0:T(8,128)(2,1)} %param.26) | copy-start | bytes 1179652
  6.5 90.0 %all-gather.6.cloned.1.call-start = ((), (), s32[]{:S(2)}) async-start(), calls=%async_computation | async-start | bytes 2113536 | tf_op jit(solution)/shard_map/all_gather | solution.py:84
  7.3 172.3 %all-gather.8.cloned.1.call-start = ((), (), s32[]{:S(2)}) async-start(), calls=%async_computation.1 | async-start | bytes 2113536 | tf_op jit(solution)/shard_map/all_gather | solution.py:85
  8.0 320.0 %all-gather.12.cloned.1.call-start = ((), (), s32[]{:S(2)}) async-start(), calls=%async_computation.3 | async-start | bytes 2621440 | tf_op jit(solution)/shard_map/all_gather | solution.py:21
  96.6 83.1 %copy-start.1 = (bf16[2,16,16,512]{3,2,1,0:T(8,128)(2,1)S(1)}, bf16[2,16,16,512]{3,2,1,0:T(8,128)(2,1)}, u32[]{:S(2)}) copy-start(bf16[2,16,16,512]{3,2,1,0:T(8,128)(2,1)} %param.19) | copy-start | bytes 1572868
  96.6 83.1 %copy-start.5 = (f32[1,512]{1,0:T(1,128)S(1)}, f32[1,512]{1,0:T(1,128)}, u32[]{:S(2)}) copy-start(f32[1,512]{1,0:T(1,128)} %param.25) | copy-start | bytes 6148
  96.6 83.1 %copy-start.6 = (f32[1,512]{1,0:T(1,128)S(1)}, f32[1,512]{1,0:T(1,128)}, u32[]{:S(2)}) copy-start(f32[1,512]{1,0:T(1,128)} %param.22) | copy-start | bytes 6148
  190.0 7.9 %collective-permute-start = (bf16[16,16,512]{2,1,0:T(8,128)(2,1)}, bf16[16,16,512]{2,1,0:T(8,128)(2,1)S(1)}, u32[]{:S(2)}, u32[]{:S(2)}) collective-permute-start(bf16[16,16,512]{2,1,0:T(8,128)(2,1)} %get-tuple-element.507), channel_id=1, source_target_pairs={{0,128},{128,256},{256,384},{1,129},{129,257},{257,385},{2,130},{1... | collective-permute-start | bytes 786440 | tf_op jit(solution)/shard_map/while/body/eval_jaxpr/ppermute | solution.py:16
  208.2 10.1 %collective-permute-start = (bf16[16,16,512]{2,1,0:T(8,128)(2,1)}, bf16[16,16,512]{2,1,0:T(8,128)(2,1)S(1)}, u32[]{:S(2)}, u32[]{:S(2)}) collective-permute-start(bf16[16,16,512]{2,1,0:T(8,128)(2,1)} %get-tuple-element.507), channel_id=1, source_target_pairs={{0,128},{128,256},{256,384},{1,129},{129,257},{257,385},{2,130},{1... | collective-permute-start | bytes 786440 | tf_op jit(solution)/shard_map/while/body/eval_jaxpr/ppermute | solution.py:16
  219.1 18.7 %collective-permute-start = (bf16[16,16,512]{2,1,0:T(8,128)(2,1)}, bf16[16,16,512]{2,1,0:T(8,128)(2,1)S(1)}, u32[]{:S(2)}, u32[]{:S(2)}) collective-permute-start(bf16[16,16,512]{2,1,0:T(8,128)(2,1)} %get-tuple-element.507), channel_id=1, source_target_pairs={{0,128},{128,256},{256,384},{1,129},{129,257},{257,385},{2,130},{1... | collective-permute-start | bytes 786440 | tf_op jit(solution)/shard_map/while/body/eval_jaxpr/ppermute | solution.py:16
  238.6 8.5 %collective-permute-start = (bf16[16,16,512]{2,1,0:T(8,128)(2,1)}, bf16[16,16,512]{2,1,0:T(8,128)(2,1)S(1)}, u32[]{:S(2)}, u32[]{:S(2)}) collective-permute-start(bf16[16,16,512]{2,1,0:T(8,128)(2,1)} %get-tuple-element.507), channel_id=1, source_target_pairs={{0,128},{128,256},{256,384},{1,129},{129,257},{257,385},{2,130},{1... | collective-permute-start | bytes 786440 | tf_op jit(solution)/shard_map/while/body/eval_jaxpr/ppermute | solution.py:16
  247.9 16.4 %collective-permute-start = (bf16[16,16,512]{2,1,0:T(8,128)(2,1)}, bf16[16,16,512]{2,1,0:T(8,128)(2,1)S(1)}, u32[]{:S(2)}, u32[]{:S(2)}) collective-permute-start(bf16[16,16,512]{2,1,0:T(8,128)(2,1)} %get-tuple-element.507), channel_id=1, source_target_pairs={{0,128},{128,256},{256,384},{1,129},{129,257},{257,385},{2,130},{1... | collective-permute-start | bytes 786440 | tf_op jit(solution)/shard_map/while/body/eval_jaxpr/ppermute | solution.py:16
  265.2 172.1 %all-gather.10.cloned.1.call-start = ((), (), s32[]{:S(2)}) async-start(), calls=%async_computation.2 | async-start | bytes 6144000 | tf_op jit(solution)/shard_map/all_gather | solution.py:153
  318.0 6.0 %copy-start.4 = (bf16[196,256]{1,0:T(8,128)(2,1)S(1)}, bf16[196,256]{1,0:T(8,128)(2,1)}, u32[]{:S(2)}) copy-start(bf16[196,256]{1,0:T(8,128)(2,1)} %param.28) | copy-start | bytes 301060
  318.0 6.7 %copy-start.7 = (f32[2,1024]{1,0:T(2,128)S(1)}, f32[2,1024]{1,0:T(2,128)}, u32[]{:S(2)}) copy-start(f32[2,1024]{1,0:T(2,128)} %param.31) | copy-start | bytes 24580
  374.2 3.1 copy-start.2
  451.4 1.0 copy-start.3
  451.4 28.0 %copy-start.8 = (s32[1,4]{1,0:T(1,128)S(1)}, s32[1,4]{1,0:T(1,128)}, u32[]{:S(2)}) copy-start(s32[1,4]{1,0:T(1,128)} %param.33) | copy-start | bytes 52
  470.5 10.9 %collective-permute-start.1 = (f32[1,1024]{1,0:T(1,128)S(1)}, f32[1,1024]{1,0:T(1,128)S(1)}, u32[]{:S(2)}, u32[]{:S(2)}) collective-permute-start(f32[1,1024]{1,0:T(1,128)S(1)} %get-tuple-element.394), channel_id=1, source_target_pairs={{0,1},{1,2},{2,3},{3,4},{4,5},{5,6},{6,7},{7,8},{8,9},{9,10},{10,1... | collective-permute-start | bytes 12296 | tf_op jit(solution)/shard_map/ppermute | solution.py:29
  472.4 9.0 %collective-permute-start.2 = (f32[1,1024]{1,0:T(1,128)S(1)}, f32[1,1024]{1,0:T(1,128)S(1)}, u32[]{:S(2)}, u32[]{:S(2)}) collective-permute-start(f32[1,1024]{1,0:T(1,128)S(1)} %get-tuple-element.393), channel_id=1, source_target_pairs={{1,0},{2,1},{3,2},{4,3},{5,4},{6,5},{7,6},{8,7},{9,8},{10,9},{11,1... | collective-permute-start | bytes 12296 | tf_op jit(solution)/shard_map/ppermute | solution.py:32
Sparse Core Ops, SparseCore 0:
  10.5 86.0 all-gather.5
  99.7 79.7 all-gather.7
  265.3 44.5 all-gather.11
  377.4 59.8 all-gather.9
